TPU v7x, 32 devices: a whole 2x2x4 slice. The times are simulated.
32 devices in a mesh: blk: 8 (over z, core), tenant: 4 (over y, x).
Axes of the slice: x: 2, y: 2, z: 4, core: 2. Of those that a mesh axis runs over, the one named last changes fastest.
Arguments:
- history_u: bfloat16 [4, 1024, 4096], P('tenant', 'blk'), may hold values from -6 to 6
- span_gate: bfloat16 [4, 64, 4096], P('tenant', 'blk'), may hold values from -6 to 6
- span_key: bfloat16 [4, 64, 4096], P('tenant', 'blk'), may hold values from -6 to 6
- span_value: bfloat16 [4, 64, 4096], P('tenant', 'blk'), may hold values from -6 to 6
- filter_taps: bfloat16 [1088, 256], P(('blk', 'tenant'))
- skip_bias: bfloat16 [4096], P(('blk', 'tenant')), may hold values from -6 to 6
- lengths: int32 [4], P('tenant'), may hold values from 1 to 1024, as said below
- page_owner: int32 [4, 8, 1], P('tenant'), may hold values from 0 to 7; in each aligned block of 8 rows (0 to 7, 8 to 15, ..., all dimensions but the last counted through in order) at most 2 rows name the same one
Outputs:
- mixed: bfloat16 [4, 64, 4096], P('tenant', 'blk')
- new_pool: bfloat16 [4, 128, 4096], P('tenant', 'blk')
Inputs may be any that keep to these rules, and one draw needn't show every extreme that they name: `lengths`: lengths are at least 1, and some tenant uses all 1024 cached positions in every draw. `page_owner`: among the 8 pages of one tenant no device is named more than 2 times, and some device is named exactly 2 times.
All inputs are finite; a program needn't handle non-finite values.
Results may differ from a plain program's by a relative error of at most 0.0044.
Values may be sent and summed in bfloat16 or wider, within the bound.
No kernel may reach another device: no remote copies, remote signals or barrier semaphores. Data moves between devices by JAX's collectives and lax.ppermute only.
A program may use at most 128 MiB of HBM per device.

v0:
```python
import jax
import jax.numpy as jnp
from jax import lax
from jax.sharding import PartitionSpec as P

PAGE = 8
PAGES_DEV = 1
MOST = 2


def toeplitz(window, tile_rows, groups):
    reversed_taps = jnp.transpose(window[::-1])
    repeated = jnp.tile(reversed_taps, (1, tile_rows))
    trimmed = repeated[:, tile_rows - 1 : tile_rows - 1 + tile_rows * (2 * tile_rows - 2)]
    return trimmed.reshape(groups, tile_rows, 2 * tile_rows - 2)[:, :, :tile_rows]


def tile_table(padded_filter, starts, tile_rows, groups):

    def one_window(start):
        window = lax.dynamic_slice_in_dim(padded_filter, start, 2 * tile_rows - 1, 0)
        return toeplitz(window, tile_rows, groups)

    return jax.vmap(one_window)(starts)


def blocked_convolution(table, sources_reversed, target_blocks, source_blocks):

    def per_target(target_index):
        tiles = lax.dynamic_slice_in_dim(table, target_index, source_blocks, 0)
        return jnp.einsum(
            "mgab,mbgc->agc", tiles, sources_reversed, preferred_element_type=jnp.float32
        )

    return lax.map(per_target, jnp.arange(target_blocks, dtype=jnp.int32))


def per_device(
    history_u, span_gate, span_key, span_value, filter_taps, skip_bias, lengths, page_owner
):
    cycle_size = lax.axis_size("blk")
    own_index = lax.axis_index("blk")
    history = history_u[0]
    gate_rows = span_gate[0]
    history_rows, width = history.shape
    span_rows = gate_rows.shape[0]
    span_total = span_rows * cycle_size
    groups = filter_taps.shape[1]
    group_size = width // groups
    taps_all, bias_all = (
        lax.all_gather(filter_taps, ("blk", "tenant"), axis=0, tiled=True),
        lax.all_gather(skip_bias, ("blk", "tenant"), axis=0, tiled=True),
    )
    length = lengths[0]
    own_rows = (span_key[0].astype(jnp.float32) * span_value[0].astype(jnp.float32)).astype(
        jnp.bfloat16
    )
    tile_rows = min(32, history_rows, span_total)
    target_blocks = span_total // tile_rows
    column_history, column_span = (
        lax.all_to_all(history, "blk", split_axis=1, concat_axis=0, tiled=True),
        lax.all_to_all(own_rows, "blk", split_axis=1, concat_axis=0, tiled=True),
    )
    column_width = width // cycle_size
    local_groups = column_width // group_size
    full_rows = column_history.shape[0]
    filter_rows_all = full_rows + span_total
    taps_local = lax.dynamic_slice_in_dim(taps_all, own_index * local_groups, local_groups, 1)
    masked_columns = jnp.where(
        jnp.arange(full_rows, dtype=jnp.int32)[:, None] < length,
        column_history,
        jnp.zeros_like(column_history),
    )
    sequence = jnp.concatenate(
        [masked_columns, jnp.zeros((span_total, column_width), jnp.bfloat16)], axis=0
    )
    sequence = lax.dynamic_update_slice(sequence, column_span, (length, jnp.int32(0)))
    source_blocks = filter_rows_all // tile_rows
    padded_filter = jnp.concatenate(
        [jnp.zeros((filter_rows_all, local_groups), jnp.bfloat16), taps_local], axis=0
    )
    offsets = jnp.arange(target_blocks + source_blocks - 1, dtype=jnp.int32) - (source_blocks - 1)
    starts = length + offsets * tile_rows - (tile_rows - 1) + filter_rows_all
    table = tile_table(padded_filter, starts, tile_rows, local_groups)
    sources_reversed = sequence.reshape(source_blocks, tile_rows, local_groups, group_size)[::-1]
    column_out = blocked_convolution(table, sources_reversed, target_blocks, source_blocks).reshape(
        span_total, column_width
    )
    convolved = lax.all_to_all(column_out, "blk", split_axis=0, concat_axis=1, tiled=True)
    mixed = (
        gate_rows.astype(jnp.float32)
        * (convolved + bias_all.astype(jnp.float32)[None, :] * own_rows.astype(jnp.float32))
    ).astype(jnp.bfloat16)
    owners = page_owner[0, :, 0]
    page_count = owners.shape[0]
    onehot = (owners[:, None] == jnp.arange(cycle_size, dtype=jnp.int32)[None, :]).astype(jnp.int32)
    before = jnp.cumsum(onehot, axis=0) - onehot
    slot_rank = jnp.sum(before * onehot, axis=1)
    selector = (
        (owners[None, :] == own_index)
        & (slot_rank[None, :] == jnp.arange(MOST, dtype=jnp.int32)[:, None])
    ).astype(jnp.bfloat16)
    local_pages = own_rows.reshape(PAGES_DEV, PAGE * width)
    targets_of = lax.dynamic_slice_in_dim(owners, own_index * PAGES_DEV, PAGES_DEV, 0)
    send_mask = targets_of[None, :] == jnp.arange(cycle_size, dtype=jnp.int32)[:, None]
    outgoing = jnp.where(
        send_mask[:, :, None], local_pages[None, :, :], jnp.zeros((), jnp.bfloat16)
    )
    incoming = lax.all_to_all(outgoing, "blk", split_axis=0, concat_axis=0, tiled=True)
    arrived = incoming.reshape(page_count, PAGE * width)
    new_pool = jnp.dot(selector, arrived, preferred_element_type=jnp.float32).astype(jnp.bfloat16)
    return (mixed[None], new_pool.reshape(MOST * PAGE, width)[None])


def solution(mesh):
    return jax.shard_map(
        per_device,
        mesh=mesh,
        in_specs=(
            P("tenant", "blk", None),
            P("tenant", "blk", None),
            P("tenant", "blk", None),
            P("tenant", "blk", None),
            P(("blk", "tenant"), None),
            P(("blk", "tenant")),
            P("tenant"),
            P("tenant", None, None),
        ),
        out_specs=(P("tenant", "blk", None), P("tenant", "blk", None)),
        check_vma=False,
    )
```

profile of v0, /device:TPU:0, one launch (start us, length us, event | category | flops | bytes accessed | tf_op | source)
XLA Modules:
  0.0 384.5 jit_solution(1890351494734139457)
XLA Ops:
  0.6 1.3 constant_dynamic-slice_fusion.1
  2.6 1.5 multiply_convert_fusion.1
  6.5 3.8 reduce
  11.4 6.3 %all-to-all-start.3 = ((bf16[8,2,16384]{2,1,0:T(2,128)(2,1)}), bf16[8,2,16384]{2,1,0:T(2,128)(2,1)S(1)}, u32[]{:S(2)}, u32[]{:S(2)}) async-start(bf16[8,2,16384]{2,1,0:T(2,128)(2,1)} %reshape.183), calls=%async_computation.3 | async-start | bytes 1048576 | tf_op jit(solution)/shard_map/all_to_all | solution.py:109
  17.8 74.8 %all-gather = bf16[32,34,256]{2,1,0:T(8,128)(2,1)S(1)} all-gather(bf16[1,34,256]{2,1,0:T(8,128)(2,1)} %bitcast.67), channel_id=1, replica_groups=mesh['blk'=8,'tenant'=4] {'blk','tenant'}, dimensions={0}, use_global_device_ids=true | all-gather | bytes 574464 | tf_op jit(solution)/shard_map/all_gather | solution.py:51
  93.4 1.3 copy.31
  95.0 3.7 all-to-all-start
  98.8 65.2 %while.12 = (s32[]{:T(128)}, bf16[2176,32]{1,0:T(8,128)(2,1)S(1)}, s32[35,2]{0,1:T(2,128)S(1)}, bf16[35,63,32]{2,1,0:T(8,128)(2,1)}, s32[]{:T(128)}) while((s32[]{:T(128)}, bf16[2176,32]{1,0:T(8,128)(2,1)S(1)}, s32[35,2]{0,1:T(2,128)S(1)}, bf16[35,63,32]{2,1,0:T(8,128)(2,1)}, s32[]{:T(128)}) %tuple.37), condition=%wide.while_cond, body=%wide.while_body.sunk | while | flops 2 | bytes 21529 | solution.py:21
  99.4 1.3 bitcast_dynamic-update-slice_fusion.2
  105.0 1.2 bitcast_dynamic-update-slice_fusion.2
  106.8 1.3 bitcast_dynamic-update-slice_fusion.2
  108.7 1.2 bitcast_dynamic-update-slice_fusion.2
  112.4 1.3 bitcast_dynamic-update-slice_fusion.2
  114.3 1.2 bitcast_dynamic-update-slice_fusion.2
  116.2 1.2 bitcast_dynamic-update-slice_fusion.2
  119.9 1.3 bitcast_dynamic-update-slice_fusion.2
  121.8 1.2 bitcast_dynamic-update-slice_fusion.2
  123.6 1.2 bitcast_dynamic-update-slice_fusion.2
  127.3 1.3 bitcast_dynamic-update-slice_fusion.2
  131.1 1.2 bitcast_dynamic-update-slice_fusion.2
  134.8 1.3 bitcast_dynamic-update-slice_fusion.2
  138.5 1.3 bitcast_dynamic-update-slice_fusion.2
  144.1 1.2 bitcast_dynamic-update-slice_fusion.2
  147.8 1.3 bitcast_dynamic-update-slice_fusion.2
  149.7 1.3 bitcast_dynamic-update-slice_fusion.2
  151.6 1.2 bitcast_dynamic-update-slice_fusion.2
  155.3 1.2 bitcast_dynamic-update-slice_fusion.2
  157.1 1.2 bitcast_dynamic-update-slice_fusion.2
  162.7 1.2 bitcast_dynamic-update-slice_fusion.2
  164.0 2.3 rev.6
  166.6 4.7 %tile.4 = bf16[35,32,32,63]{3,2,1,0:T(8,128)(2,1)} broadcast(bf16[35,32,63]{2,1,0:T(8,128)(2,1)S(1)} %copy.30), dimensions={0,1,3} | broadcast | bytes 4656960 | tf_op jit(solution)/shard_map/vmap()/tile | solution.py:13
  171.3 16.1 %tile.10 = bf16[35,32,2016]{2,1,0:T(8,128)(2,1)} reshape(bf16[35,32,32,63]{3,2,1,0:T(8,128)(2,1)} %tile.4) | data formatting | bytes 9031680 | tf_op jit(solution)/shard_map/vmap()/tile | solution.py:13
  187.4 6.9 %slice.19 = bf16[35,32,1984]{2,1,0:T(8,128)(2,1)} slice(bf16[35,32,2016]{2,1,0:T(8,128)(2,1)} %tile.10), slice={[0:35], [0:32], [31:2015]} | slice | bytes 8888320 | tf_op jit(solution)/shard_map/vmap()/slice | solution.py:14
  194.4 31.4 %reshape.155 = bf16[35,32,32,62]{3,2,1,0:T(8,128)(2,1)} reshape(bf16[35,32,1984]{2,1,0:T(8,128)(2,1)} %slice.19) | data formatting | bytes 8888320 | tf_op jit(solution)/shard_map/vmap()/reshape | solution.py:15
  225.8 14.3 %copy.34 = bf16[35,32,32,32]{0,2,3,1:T(8,128)(2,1)} copy(bf16[35,32,32,32]{3,2,1,0:T(8,128)(2,1)} %bitcast.60) | data formatting | bytes 4587520 | tf_op jit(solution)/shard_map/while | solution.py:35
  240.1 66.1 %all-gather.1 = bf16[32,1,128]{2,1,0:T(2,128)(2,1)S(1)} all-gather(bf16[1,1,128]{2,1,0:T(2,128)(2,1)S(1)} %bitcast.70), channel_id=1, replica_groups=mesh['blk'=8,'tenant'=4] {'blk','tenant'}, dimensions={0}, use_global_device_ids=true | all-gather | bytes 8448 | tf_op jit(solution)/shard_map/all_gather | solution.py:52
  307.1 3.6 all-to-all-start.1
  311.5 4.8 %all-to-all-done.1 = bf16[8,8,512]{2,0,1:T(8,128)(2,1)S(1)} async-done(((bf16[8,8,512]{2,0,1:T(8,128)(2,1)}), bf16[8,8,512]{2,0,1:T(8,128)(2,1)S(1)}, u32[]{:S(2)}, u32[]{:S(2)}) %all-to-all-start.1) | async-done | bytes 65568 | tf_op jit(solution)/shard_map/all_to_all | solution.py:62
  317.4 4.8 %reshape.156 = bf16[34,32,32,16]{1,0,3,2:T(8,128)(2,1)} reshape(bf16[1088,512]{0,1:T(8,128)(2,1)S(1)} %copy.33) | data formatting | bytes 2228224 | tf_op jit(solution)/shard_map/reshape | solution.py:85
  322.2 20.3 %rev.7 = bf16[34,32,32,16]{1,0,3,2:T(8,128)(2,1)} reverse(bf16[34,32,32,16]{1,0,3,2:T(8,128)(2,1)} %reshape.156), dimensions={0} | reverse | bytes 2228224 | tf_op jit(solution)/shard_map/rev | solution.py:85
  342.5 8.7 %copy.35 = bf16[34,32,32,16]{0,3,1,2:T(8,128)(2,1)} copy(bf16[34,32,32,16]{1,0,3,2:T(8,128)(2,1)} %rev.7) | data formatting | bytes 2228224 | tf_op jit(solution)/shard_map/while | solution.py:35
  351.2 19.5 %while.11 = (s32[]{:T(128)}, f32[2,32,32,16]{1,3,2,0:T(8,128)S(1)}, s32[2]{0:T(128)S(1)}, bf16[35,32,32,32]{0,2,3,1:T(8,128)(2,1)}, bf16[34,32,32,16]{0,3,1,2:T(8,128)(2,1)}, /*index=5*/s32[]{:T(128)}, s32[]{:T(128)}, s32[]{:T(128)}) while((s32[]{:T(128)}, f32[2,32,32,16]{1,3,2,0:T(8,128)S(1)}, s32[2]{0:T(128)S(1)}, ...), condition=%wide.region_1.2_spmd, body=%wide.region_0.1_spmd.sunk | while | flops 35651588 | bytes 3670155 | solution.py:35
  354.0 7.0 %fusion.23 = f32[2,32,32,16]{1,3,2,0:T(8,128)S(1)} fusion(f32[2,32,32,16]{1,3,2,0:T(8,128)S(1)} %get-tuple-element.156, s32[]{:T(128)} %get-tuple-element.155, bf16[34,32,32,16]{0,3,1,2:T(8,128)(2,1)} %get-tuple-element.167, bf16[35,32,32,32]{0,2,3,1:T(8,128)(2,1)} %get-tuple-element.166, s32[]{:T(128)S(6)} %select_n.48), kind=kOutput, calls=%fused_computation.3.clone.1 | convolution fusion | flops 35651584 | bytes 3670024 | tf_op jit(solution)/shard_map/while/body/eval_jaxpr/mgab,mbgc->agc/dot_general | solution.py:31
  363.7 7.0 %fusion.23 = f32[2,32,32,16]{1,3,2,0:T(8,128)S(1)} fusion(f32[2,32,32,16]{1,3,2,0:T(8,128)S(1)} %get-tuple-element.156, s32[]{:T(128)} %get-tuple-element.155, bf16[34,32,32,16]{0,3,1,2:T(8,128)(2,1)} %get-tuple-element.167, bf16[35,32,32,32]{0,2,3,1:T(8,128)(2,1)} %get-tuple-element.166, s32[]{:T(128)S(6)} %select_n.48), kind=kOutput, calls=%fused_computation.3.clone.1 | convolution fusion | flops 35651584 | bytes 3670024 | tf_op jit(solution)/shard_map/while/body/eval_jaxpr/mgab,mbgc->agc/dot_general | solution.py:31
  371.6 1.3 all_to_all.50
  372.9 3.4 all-to-all-start.2
  377.7 5.3 %all-to-all-done.2 = f32[8,8,512]{2,1,0:T(8,128)S(1)} async-done(((f32[8,8,512]{2,1,0:T(8,128)}), f32[8,8,512]{2,1,0:T(8,128)S(1)}, u32[]{:S(2)}, u32[]{:S(2)}) %all-to-all-start.2) | async-done | bytes 131104 | tf_op jit(solution)/shard_map/all_to_all | solution.py:89
  383.0 1.5 multiply_convert_fusion
  (127 shorter events, 50.2 us)
Async XLA Ops:
  0.6 92.8 %copy-start = (bf16[1,128,4096]{2,1,0:T(8,128)(2,1)S(1)}, bf16[1,128,4096]{2,1,0:T(8,128)(2,1)}, u32[]{:S(2)}) copy-start(bf16[1,128,4096]{2,1,0:T(8,128)(2,1)} %param.10) | copy-start | bytes 3145732
  11.4 83.6 %all-to-all-start.3 = ((bf16[8,2,16384]{2,1,0:T(2,128)(2,1)}), bf16[8,2,16384]{2,1,0:T(2,128)(2,1)S(1)}, u32[]{:S(2)}, u32[]{:S(2)}) async-start(bf16[8,2,16384]{2,1,0:T(2,128)(2,1)} %reshape.183), calls=%async_computation.3 | async-start | bytes 1048576 | tf_op jit(solution)/shard_map/all_to_all | solution.py:109
  95.0 212.0 %all-to-all-start = ((bf16[128,8,512]{0,2,1:T(8,128)(2,1)}), bf16[128,8,512]{0,2,1:T(8,128)(2,1)S(1)}, u32[]{:S(2)}, u32[]{:S(2)}) async-start(bf16[128,8,512]{0,2,1:T(8,128)(2,1)} %bitcast.8), calls=%async_computation | async-start | bytes 2097152 | tf_op jit(solution)/shard_map/all_to_all | solution.py:61
  225.8 14.3 %copy-start.4 = (bf16[128]{0:T(256)(128)(2,1)S(1)}, bf16[128]{0:T(256)(128)(2,1)}, u32[]{:S(2)}) copy-start(bf16[128]{0:T(256)(128)(2,1)} %param.15) | copy-start | bytes 772
  225.8 80.4 %copy-start.3 = (s32[1,8,1]{1,2,0:T(1,128)S(1)}, s32[1,8,1]{1,2,0:T(1,128)}, u32[]{:S(2)}) copy-start(s32[1,8,1]{1,2,0:T(1,128)} %param.17) | copy-start | bytes 100
  307.1 9.2 %all-to-all-start.1 = ((bf16[8,8,512]{2,0,1:T(8,128)(2,1)}), bf16[8,8,512]{2,0,1:T(8,128)(2,1)S(1)}, u32[]{:S(2)}, u32[]{:S(2)}) async-start(bf16[8,8,512]{2,0,1:T(8,128)(2,1)} %bitcast.11), calls=%async_computation.1 | async-start | bytes 131072 | tf_op jit(solution)/shard_map/all_to_all | solution.py:62
  342.5 8.7 %copy-start.1 = (f32[2,32,32,16]{1,3,2,0:T(8,128)S(1)}, f32[2,32,32,16]{1,3,2,0:T(8,128)}, u32[]{:S(2)}) copy-start(f32[2,32,32,16]{1,3,2,0:T(8,128)} %custom-call) | copy-start | bytes 393220
  351.2 31.8 %copy-start.2 = (bf16[1,8,4096]{2,1,0:T(8,128)(2,1)S(1)}, bf16[1,8,4096]{2,1,0:T(8,128)(2,1)}, u32[]{:S(2)}) copy-start(bf16[1,8,4096]{2,1,0:T(8,128)(2,1)} %param.11) | copy-start | bytes 196612
  372.9 10.1 %all-to-all-start.2 = ((f32[8,8,512]{2,1,0:T(8,128)}), f32[8,8,512]{2,1,0:T(8,128)S(1)}, u32[]{:S(2)}, u32[]{:S(2)}) async-start(f32[8,8,512]{2,1,0:T(8,128)} %all_to_all.50), calls=%async_computation.2 | async-start | bytes 262144 | tf_op jit(solution)/shard_map/all_to_all | solution.py:89
where the time goes:
time: 387 us; the launch traced here: 385 us
  local copies, waits for them, and re-layouts  187 us (48%)
  blocking collectives  141 us (36%)
  starting transfers between devices  17 us (4%)
  matrix products  14.7 us (4%)
  waiting for transfers between devices  10.1 us (3%)
  other arithmetic  8.95 us (2%)
  loops' own time  4.23 us (1%)
    all_gather x1, blocking collectives, per_device(): lax.all_gather(filter_taps, ('blk', 'tenant'), axis=0, tiled=True)  74.8 us
    all_gather x1, blocking collectives, per_device(): lax.all_gather(skip_bias, ('blk', 'tenant'), axis=0, tiled=True)  66.1 us
    gather x105, local copies, waits for them, and re-layouts  65.1 us
    reshape x1, local copies, waits for them, and re-layouts, toeplitz(): trimmed.reshape(groups, tile_rows, 2 * tile_rows - 2)[:, :, :tile_rows]  31.4 us
    while x3, local copies, waits for them, and re-layouts, blocked_convolution(): return lax.map(per_target, jnp.arange(target_blocks, dtype=jnp.int32))  23.9 us
    another operation x2, local copies, waits for them, and re-layouts, toeplitz(): repeated = jnp.tile(reversed_taps, (1, tile_rows))  20.8 us
    rev x1, local copies, waits for them, and re-layouts, per_device(): sequence.reshape(source_blocks, tile_rows, local_groups, group_size)[::-1]  20.3 us
    dot_general x2, matrix products, per_target(): jnp.einsum('mgab,mbgc->agc', tiles, sources_reversed, preferred_element_t...  14 us
  transfers between devices with their start and end apart: 4, of which 2 were waited for; matrix products, arithmetic and copies ran while one was open for 38% of the time, Pallas kernels for 0%

commit v1 on v0

--- a/solution.py
+++ b/solution.py
@@ -6,6 +6,28 @@
 PAGE = 8
 PAGES_DEV = 1
 MOST = 2
+
+
+def in_order(tiles, dim):
+    dims = list(tiles.shape[1:])
+    dims[dim] *= tiles.shape[0]
+    return jnp.moveaxis(tiles, 0, dim).reshape(dims)
+
+
+def grow_blocks(x, axis):
+    length = lax.axis_size(axis)
+    blocks = x[None]
+    for level in range(length.bit_length() - 1):
+        stride = 1 << level
+        received = lax.ppermute(blocks, axis, [(i, i ^ stride) for i in range(length)])
+        both = jnp.stack([blocks, received])
+        upper = lax.axis_index(axis) >> level & 1
+        blocks = jnp.where(upper == 0, both, both[::-1]).reshape(-1, *x.shape)
+    return blocks
+
+
+def doubled_up(value, axis, dim):
+    return in_order(grow_blocks(value, axis), dim)
 
 
 def toeplitz(window, tile_rows, groups):
@@ -49,7 +71,7 @@
     group_size = width // groups
     taps_all, bias_all = (
         lax.all_gather(filter_taps, ("blk", "tenant"), axis=0, tiled=True),
-        lax.all_gather(skip_bias, ("blk", "tenant"), axis=0, tiled=True),
+        doubled_up(skip_bias, ("blk", "tenant"), 0),
     )
     length = lengths[0]
     own_rows = (span_key[0].astype(jnp.float32) * span_value[0].astype(jnp.float32)).astype(

time: 387 us -> 344 us (0.89)
  blocking collectives: 141 us -> 74.8 us
  waiting for transfers between devices: 10.1 us -> 25.6 us
  starting transfers between devices: 17 us -> 25.2 us
    all_gather x1 -> x0, blocking collectives: 66.1 us -> none  [per_device(): lax.all_gather(skip_bias, ('blk', 'tenant'), axis=0, tiled=True)]
    ppermute x0 -> x5, waiting for transfers between devices: none -> 15.5 us  [grow_blocks(): lax.ppermute(blocks, axis, [(i, i ^ stride) for i in range(length)])]
    ppermute x0 -> x5, starting transfers between devices: none -> 9.64 us  [grow_blocks(): lax.ppermute(blocks, axis, [(i, i ^ stride) for i in range(length)])]
  transfers between devices with their start and end apart: 4 -> 9, of which waited for: 2 -> 4; matrix products, arithmetic and copies ran while one was open for 38% -> 46% of each run, Pallas kernels for 0% -> 0%
where the time goes in v1:
time: 344 us; the launch traced here: 342 us
  local copies, waits for them, and re-layouts  187 us (54%)
  blocking collectives  74.8 us (22%)
  waiting for transfers between devices  25.6 us (7%)
  starting transfers between devices  25.2 us (7%)
  matrix products  14.7 us (4%)
  other arithmetic  9.01 us (3%)
  loops' own time  3.9 us (1%)
    all_gather x1, blocking collectives, per_device(): lax.all_gather(filter_taps, ('blk', 'tenant'), axis=0, tiled=True)  74.8 us
    gather x105, local copies, waits for them, and re-layouts  65.1 us
    reshape x1, local copies, waits for them, and re-layouts, toeplitz(): trimmed.reshape(groups, tile_rows, 2 * tile_rows - 2)[:, :, :tile_rows]  31.4 us
    while x3, local copies, waits for them, and re-layouts, blocked_convolution(): return lax.map(per_target, jnp.arange(target_blocks, dtype=jnp.int32))  23.9 us
    another operation x2, local copies, waits for them, and re-layouts, toeplitz(): repeated = jnp.tile(reversed_taps, (1, tile_rows))  20.9 us
    rev x1, local copies, waits for them, and re-layouts, per_device(): sequence.reshape(source_blocks, tile_rows, local_groups, group_size)[::-1]  20.2 us
    ppermute x5, waiting for transfers between devices, grow_blocks(): lax.ppermute(blocks, axis, [(i, i ^ stride) for i in range(length)])  15.5 us
    dot_general x2, matrix products, per_target(): jnp.einsum('mgab,mbgc->agc', tiles, sources_reversed, preferred_element_t...  14 us
  transfers between devices with their start and end apart: 9, of which 4 were waited for; matrix products, arithmetic and copies ran while one was open for 46% of the time, Pallas kernels for 0%

profile of v1, /device:TPU:0, one launch (start us, length us, event | category | flops | bytes accessed | tf_op | source)
XLA Modules:
  0.0 341.6 jit_solution(15793917632358611750)
XLA Ops:
  0.6 3.0 collective-permute-start
  5.5 1.5 multiply_convert_fusion.1
  9.4 3.8 %reduce = bf16[8,32768]{1,0:T(8,128)(2,1)S(1)} reduce(bf16[8,1,32768]{2,1,0:T(2,128)(2,1)S(1)} %broadcast_select_fusion, bf16[]{:T(256)} %broadcast.143), dimensions={1}, to_apply=%broadcast_select_fusion.reduce_sub_computation | reduce | bytes 1048578 | tf_op jit(solution)/shard_map/jit(_where)/select_n | solution.py:128
  14.4 4.9 %all-to-all-start.3 = ((bf16[8,2,16384]{2,1,0:T(2,128)(2,1)}), bf16[8,2,16384]{2,1,0:T(2,128)(2,1)S(1)}, u32[]{:S(2)}, u32[]{:S(2)}) async-start(bf16[8,2,16384]{2,1,0:T(2,128)(2,1)} %reshape.203), calls=%async_computation.3 | async-start | bytes 1048576 | tf_op jit(solution)/shard_map/all_to_all | solution.py:131
  19.3 74.8 %all-gather = bf16[32,34,256]{2,1,0:T(8,128)(2,1)S(1)} all-gather(bf16[1,34,256]{2,1,0:T(8,128)(2,1)} %bitcast.87), channel_id=1, replica_groups=mesh['blk'=8,'tenant'=4] {'blk','tenant'}, dimensions={0}, use_global_device_ids=true | all-gather | bytes 574464 | tf_op jit(solution)/shard_map/all_gather | solution.py:73
  95.2 65.2 %while.12 = (s32[]{:T(128)}, bf16[2176,32]{1,0:T(8,128)(2,1)S(1)}, s32[35,2]{0,1:T(2,128)S(1)}, bf16[35,63,32]{2,1,0:T(8,128)(2,1)}, s32[]{:T(128)}) while((s32[]{:T(128)}, bf16[2176,32]{1,0:T(8,128)(2,1)S(1)}, s32[35,2]{0,1:T(2,128)S(1)}, bf16[35,63,32]{2,1,0:T(8,128)(2,1)}, s32[]{:T(128)}) %tuple.40), condition=%wide.while_cond, body=%wide.while_body.sunk | while | flops 2 | bytes 21529 | solution.py:43
  97.7 1.2 bitcast_dynamic-update-slice_fusion.2
  99.6 1.2 bitcast_dynamic-update-slice_fusion.2
  101.4 1.2 bitcast_dynamic-update-slice_fusion.2
  105.1 1.2 bitcast_dynamic-update-slice_fusion.2
  107.0 1.2 bitcast_dynamic-update-slice_fusion.2
  108.9 1.2 bitcast_dynamic-update-slice_fusion.2
  112.6 1.2 bitcast_dynamic-update-slice_fusion.2
  116.3 1.2 bitcast_dynamic-update-slice_fusion.2
  120.1 1.2 bitcast_dynamic-update-slice_fusion.2
  123.8 1.2 bitcast_dynamic-update-slice_fusion.2
  129.4 1.2 bitcast_dynamic-update-slice_fusion.2
  133.1 1.2 bitcast_dynamic-update-slice_fusion.2
  134.9 1.2 bitcast_dynamic-update-slice_fusion.2
  136.8 1.2 bitcast_dynamic-update-slice_fusion.2
  140.5 1.2 bitcast_dynamic-update-slice_fusion.2
  142.4 1.2 bitcast_dynamic-update-slice_fusion.2
  146.1 1.2 bitcast_dynamic-update-slice_fusion.2
  148.0 1.2 bitcast_dynamic-update-slice_fusion.2
  151.7 1.2 bitcast_dynamic-update-slice_fusion.2
  160.4 1.3 copy.31
  161.9 3.7 %all-to-all-start = ((bf16[128,8,512]{0,2,1:T(8,128)(2,1)}), bf16[128,8,512]{0,2,1:T(8,128)(2,1)S(1)}, u32[]{:S(2)}, u32[]{:S(2)}) async-start(bf16[128,8,512]{0,2,1:T(8,128)(2,1)} %bitcast.8), calls=%async_computation | async-start | bytes 2097152 | tf_op jit(solution)/shard_map/all_to_all | solution.py:83
  166.9 1.8 collective-permute-start.3
  168.9 14.6 %collective-permute-done.3 = bf16[8,128]{1,0:T(8,128)(2,1)S(1)} collective-permute-done((bf16[8,128]{1,0:T(8,128)(2,1)S(1)}, bf16[8,128]{1,0:T(8,128)(2,1)S(1)}, u32[]{:S(2)}, u32[]{:S(2)}) %collective-permute-start.3) | collective-permute-done | bytes 2080 | tf_op jit(solution)/shard_map/ppermute | solution.py:22
  183.5 4.5 %collective-permute-start.4 = (bf16[16,128]{1,0:T(8,128)(2,1)S(1)}, bf16[16,128]{1,0:T(8,128)(2,1)S(1)}, u32[]{:S(2)}, u32[]{:S(2)}) collective-permute-start(bf16[16,128]{1,0:T(8,128)(2,1)S(1)} %get-tuple-element.77), channel_id=1, source_target_pairs={{0,16},{1,17},{2,18},{3,19},{4,20},{5,21},{6,22},{7,23},{8,24},{9,... | collective-permute-start | bytes 12296 | tf_op jit(solution)/shard_map/ppermute | solution.py:22
  188.0 2.3 rev.21
  190.6 4.7 %tile.4 = bf16[35,32,32,63]{3,2,1,0:T(8,128)(2,1)} broadcast(bf16[35,32,63]{2,1,0:T(8,128)(2,1)S(1)} %copy.30), dimensions={0,1,3} | broadcast | bytes 4656960 | tf_op jit(solution)/shard_map/vmap()/tile | solution.py:35
  195.4 16.1 %tile.10 = bf16[35,32,2016]{2,1,0:T(8,128)(2,1)} reshape(bf16[35,32,32,63]{3,2,1,0:T(8,128)(2,1)} %tile.4) | data formatting | bytes 9031680 | tf_op jit(solution)/shard_map/vmap()/tile | solution.py:35
  211.5 7.0 %slice.19 = bf16[35,32,1984]{2,1,0:T(8,128)(2,1)} slice(bf16[35,32,2016]{2,1,0:T(8,128)(2,1)} %tile.10), slice={[0:35], [0:32], [31:2015]} | slice | bytes 8888320 | tf_op jit(solution)/shard_map/vmap()/slice | solution.py:36
  218.4 31.4 %reshape.173 = bf16[35,32,32,62]{3,2,1,0:T(8,128)(2,1)} reshape(bf16[35,32,1984]{2,1,0:T(8,128)(2,1)} %slice.19) | data formatting | bytes 8888320 | tf_op jit(solution)/shard_map/vmap()/reshape | solution.py:37
  249.8 14.3 %copy.34 = bf16[35,32,32,32]{0,2,3,1:T(8,128)(2,1)} copy(bf16[35,32,32,32]{3,2,1,0:T(8,128)(2,1)} %bitcast.80) | data formatting | bytes 4587520 | tf_op jit(solution)/shard_map/while | solution.py:57
  264.7 3.6 %all-to-all-start.1 = ((bf16[8,8,512]{2,0,1:T(8,128)(2,1)}), bf16[8,8,512]{2,0,1:T(8,128)(2,1)S(1)}, u32[]{:S(2)}, u32[]{:S(2)}) async-start(bf16[8,8,512]{2,0,1:T(8,128)(2,1)} %bitcast.11), calls=%async_computation.1 | async-start | bytes 131072 | tf_op jit(solution)/shard_map/all_to_all | solution.py:84
  269.1 4.8 %all-to-all-done.1 = bf16[8,8,512]{2,0,1:T(8,128)(2,1)S(1)} async-done(((bf16[8,8,512]{2,0,1:T(8,128)(2,1)}), bf16[8,8,512]{2,0,1:T(8,128)(2,1)S(1)}, u32[]{:S(2)}, u32[]{:S(2)}) %all-to-all-start.1) | async-done | bytes 65568 | tf_op jit(solution)/shard_map/all_to_all | solution.py:84
  275.0 4.7 %reshape.174 = bf16[34,32,32,16]{1,0,3,2:T(8,128)(2,1)} reshape(bf16[1088,512]{0,1:T(8,128)(2,1)S(1)} %copy.33) | data formatting | bytes 2228224 | tf_op jit(solution)/shard_map/reshape | solution.py:107
  279.8 20.2 %rev.22 = bf16[34,32,32,16]{1,0,3,2:T(8,128)(2,1)} reverse(bf16[34,32,32,16]{1,0,3,2:T(8,128)(2,1)} %reshape.174), dimensions={0} | reverse | bytes 2228224 | tf_op jit(solution)/shard_map/rev | solution.py:107
  300.0 8.7 %copy.35 = bf16[34,32,32,16]{0,3,1,2:T(8,128)(2,1)} copy(bf16[34,32,32,16]{1,0,3,2:T(8,128)(2,1)} %rev.22) | data formatting | bytes 2228224 | tf_op jit(solution)/shard_map/while | solution.py:57
  308.8 19.1 %while.11 = (s32[]{:T(128)}, f32[2,32,32,16]{1,3,2,0:T(8,128)S(1)}, s32[2]{0:T(128)S(1)}, bf16[35,32,32,32]{0,2,3,1:T(8,128)(2,1)}, bf16[34,32,32,16]{0,3,1,2:T(8,128)(2,1)}, /*index=5*/s32[]{:T(128)}, s32[]{:T(128)}, s32[]{:T(128)}) while((s32[]{:T(128)}, f32[2,32,32,16]{1,3,2,0:T(8,128)S(1)}, s32[2]{0:T(128)S(1)}, ...), condition=%wide.region_1.2_spmd, body=%wide.region_0.1_spmd.sunk | while | flops 35651588 | bytes 3670155 | solution.py:57
  311.3 7.0 %fusion.25 = f32[2,32,32,16]{1,3,2,0:T(8,128)S(1)} fusion(f32[2,32,32,16]{1,3,2,0:T(8,128)S(1)} %get-tuple-element.160, s32[]{:T(128)} %get-tuple-element.159, bf16[34,32,32,16]{0,3,1,2:T(8,128)(2,1)} %get-tuple-element.171, bf16[35,32,32,32]{0,2,3,1:T(8,128)(2,1)} %get-tuple-element.170, s32[]{:T(128)S(6)} %select_n.116), kind=kOutput, calls=%fused_computation.3.clone.1 | convolution fusion | flops 35651584 | bytes 3670024 | tf_op jit(solution)/shard_map/while/body/eval_jaxpr/mgab,mbgc->agc/dot_general | solution.py:53
  320.8 7.0 %fusion.25 = f32[2,32,32,16]{1,3,2,0:T(8,128)S(1)} fusion(f32[2,32,32,16]{1,3,2,0:T(8,128)S(1)} %get-tuple-element.160, s32[]{:T(128)} %get-tuple-element.159, bf16[34,32,32,16]{0,3,1,2:T(8,128)(2,1)} %get-tuple-element.171, bf16[35,32,32,32]{0,2,3,1:T(8,128)(2,1)} %get-tuple-element.170, s32[]{:T(128)S(6)} %select_n.116), kind=kOutput, calls=%fused_computation.3.clone.1 | convolution fusion | flops 35651584 | bytes 3670024 | tf_op jit(solution)/shard_map/while/body/eval_jaxpr/mgab,mbgc->agc/dot_general | solution.py:53
  328.7 1.3 all_to_all.50
  330.0 3.4 all-to-all-start.2
  334.8 5.3 %all-to-all-done.2 = f32[8,8,512]{2,1,0:T(8,128)S(1)} async-done(((f32[8,8,512]{2,1,0:T(8,128)}), f32[8,8,512]{2,1,0:T(8,128)S(1)}, u32[]{:S(2)}, u32[]{:S(2)}) %all-to-all-start.2) | async-done | bytes 131104 | tf_op jit(solution)/shard_map/all_to_all | solution.py:111
  340.1 1.5 multiply_convert_fusion
  (147 shorter events, 55.3 us)
Async XLA Ops:
  0.6 159.8 %copy-start = (bf16[1,128,4096]{2,1,0:T(8,128)(2,1)S(1)}, bf16[1,128,4096]{2,1,0:T(8,128)(2,1)}, u32[]{:S(2)}) copy-start(bf16[1,128,4096]{2,1,0:T(8,128)(2,1)} %param.10) | copy-start | bytes 3145732
  0.6 161.1 %collective-permute-start = (bf16[1,128]{1,0:T(2,128)(2,1)}, bf16[1,128]{1,0:T(2,128)(2,1)S(1)}, u32[]{:S(2)}, u32[]{:S(2)}) collective-permute-start(bf16[1,128]{1,0:T(2,128)(2,1)} %bitcast.97), channel_id=1, source_target_pairs={{0,1},{1,0},{2,3},{3,2},{4,5},{5,4},{6,7},{7,6},{8,9},{9,8},{10,11... | collective-permute-start | bytes 776 | tf_op jit(solution)/shard_map/ppermute | solution.py:22
  7.9 153.8 %copy-start.4 = (bf16[128]{0:T(256)(128)(2,1)S(1)}, bf16[128]{0:T(256)(128)(2,1)}, u32[]{:S(2)}) copy-start(bf16[128]{0:T(256)(128)(2,1)} %param.15) | copy-start | bytes 772
  13.2 152.4 %copy-start.3 = (s32[1,8,1]{1,2,0:T(1,128)S(1)}, s32[1,8,1]{1,2,0:T(1,128)}, u32[]{:S(2)}) copy-start(s32[1,8,1]{1,2,0:T(1,128)} %param.17) | copy-start | bytes 100
  14.4 147.4 %all-to-all-start.3 = ((bf16[8,2,16384]{2,1,0:T(2,128)(2,1)}), bf16[8,2,16384]{2,1,0:T(2,128)(2,1)S(1)}, u32[]{:S(2)}, u32[]{:S(2)}) async-start(bf16[8,2,16384]{2,1,0:T(2,128)(2,1)} %reshape.203), calls=%async_computation.3 | async-start | bytes 1048576 | tf_op jit(solution)/shard_map/all_to_all | solution.py:131
  161.8 3.9 %collective-permute-start.1 = (bf16[2,128]{1,0:T(2,128)(2,1)S(1)}, bf16[2,128]{1,0:T(2,128)(2,1)S(1)}, u32[]{:S(2)}, u32[]{:S(2)}) collective-permute-start(bf16[2,128]{1,0:T(2,128)(2,1)S(1)} %bitcast.100), channel_id=1, source_target_pairs={{0,2},{1,3},{2,0},{3,1},{4,6},{5,7},{6,4},{7,5},{8,10},{9,11},{10,... | collective-permute-start | bytes 1544 | tf_op jit(solution)/shard_map/ppermute | solution.py:22
  161.9 102.8 %all-to-all-start = ((bf16[128,8,512]{0,2,1:T(8,128)(2,1)}), bf16[128,8,512]{0,2,1:T(8,128)(2,1)S(1)}, u32[]{:S(2)}, u32[]{:S(2)}) async-start(bf16[128,8,512]{0,2,1:T(8,128)(2,1)} %bitcast.8), calls=%async_computation | async-start | bytes 2097152 | tf_op jit(solution)/shard_map/all_to_all | solution.py:83
  165.7 1.2 collective-permute-start.2
  166.9 16.6 %collective-permute-start.3 = (bf16[8,128]{1,0:T(8,128)(2,1)S(1)}, bf16[8,128]{1,0:T(8,128)(2,1)S(1)}, u32[]{:S(2)}, u32[]{:S(2)}) collective-permute-start(bf16[8,128]{1,0:T(8,128)(2,1)S(1)} %bitcast.88), channel_id=1, source_target_pairs={{0,8},{1,9},{2,10},{3,11},{4,12},{5,13},{6,14},{7,15},{8,0},{9,1},... | collective-permute-start | bytes 6152 | tf_op jit(solution)/shard_map/ppermute | solution.py:22
  183.5 80.6 %collective-permute-start.4 = (bf16[16,128]{1,0:T(8,128)(2,1)S(1)}, bf16[16,128]{1,0:T(8,128)(2,1)S(1)}, u32[]{:S(2)}, u32[]{:S(2)}) collective-permute-start(bf16[16,128]{1,0:T(8,128)(2,1)S(1)} %get-tuple-element.77), channel_id=1, source_target_pairs={{0,16},{1,17},{2,18},{3,19},{4,20},{5,21},{6,22},{7,23},{8,24},{9,... | collective-permute-start | bytes 12296 | tf_op jit(solution)/shard_map/ppermute | solution.py:22
  264.7 9.2 %all-to-all-start.1 = ((bf16[8,8,512]{2,0,1:T(8,128)(2,1)}), bf16[8,8,512]{2,0,1:T(8,128)(2,1)S(1)}, u32[]{:S(2)}, u32[]{:S(2)}) async-start(bf16[8,8,512]{2,0,1:T(8,128)(2,1)} %bitcast.11), calls=%async_computation.1 | async-start | bytes 131072 | tf_op jit(solution)/shard_map/all_to_all | solution.py:84
  300.0 8.7 %copy-start.1 = (f32[2,32,32,16]{1,3,2,0:T(8,128)S(1)}, f32[2,32,32,16]{1,3,2,0:T(8,128)}, u32[]{:S(2)}) copy-start(f32[2,32,32,16]{1,3,2,0:T(8,128)} %custom-call) | copy-start | bytes 393220
  308.8 31.4 %copy-start.2 = (bf16[1,8,4096]{2,1,0:T(8,128)(2,1)S(1)}, bf16[1,8,4096]{2,1,0:T(8,128)(2,1)}, u32[]{:S(2)}) copy-start(bf16[1,8,4096]{2,1,0:T(8,128)(2,1)} %param.11) | copy-start | bytes 196612
  330.0 10.1 %all-to-all-start.2 = ((f32[8,8,512]{2,1,0:T(8,128)}), f32[8,8,512]{2,1,0:T(8,128)S(1)}, u32[]{:S(2)}, u32[]{:S(2)}) async-start(f32[8,8,512]{2,1,0:T(8,128)} %all_to_all.50), calls=%async_computation.2 | async-start | bytes 262144 | tf_op jit(solution)/shard_map/all_to_all | solution.py:111
